TPU v7x, 128 devices: a whole 4x4x4 slice. The times are simulated.
128 devices in a mesh: section: 2 (over core), cin: 8 (over z_hi, y), cout: 8 (over z_lo, x).
Axes of the slice: x: 4, y: 4, z: 4 (z_hi: 2, z_lo: 2; z = z_hi * 2 + z_lo), core: 2. Of those that a mesh axis runs over, the one named last changes fastest.
Arguments:
- inner_features: bfloat16 [2, 784, 2560], P('section', None, ('cin', 'cout')), may hold values from 0 to 2
- block_input: bfloat16 [2, 784, 5120], P('section', None, ('cin', 'cout')), may hold values from -6 to 6
- first_kernel: bfloat16 [9, 2560, 2560], P(None, 'cin', 'cout'), may hold values from -0.0546875 to 0.0546875
- expand_weight: bfloat16 [2560, 5120], P('cout', 'cin'), may hold values from -0.15625 to 0.15625
- reduce_weight: bfloat16 [5120, 5120], P(('cin', 'section'), 'cout'), may hold values from -0.125 to 0.125
- stride_kernel: bfloat16 [9, 5120, 5120], P(None, 'cout', ('section', 'cin')), may hold values from -0.0390625 to 0.0390625
- output_grad: bfloat16 [2, 196, 5120], P(None, None, ('section', 'cin', 'cout')), may hold values from -6 to 6
Outputs:
- inner_gradient: float32 [2, 784, 2560], P('section', None, ('cin', 'cout'))
- input_gradient: bfloat16 [2, 784, 5120], P('section', None, ('cin', 'cout'))
- first_gradient: float32 [9, 2560, 2560], P(None, 'cin', 'cout')
- expand_gradient: float32 [2560, 5120], P('cout', 'cin')
- reduce_gradient: float32 [5120, 5120], P(('cin', 'section'), 'cout')
- stride_gradient: float32 [9, 5120, 5120], P(None, 'cout', ('section', 'cin'))
All inputs are finite; a program needn't handle non-finite values.
Results may differ from a plain program's by a relative error of at most 0.013.
Values may be sent and summed in bfloat16 or wider, within the bound.
A program may use at most 192 MiB of HBM per device.

v0:
```python
import jax
import jax.numpy as jnp
from jax import lax
from jax.sharding import PartitionSpec as P

SIDE = 28


def smooth_gate(values):
    return values * jax.nn.sigmoid(values)


def gate_slope(values):
    logistic = jax.nn.sigmoid(values)
    return logistic * (1.0 + values * (1.0 - logistic))


def flatten_rows(images):
    return images.reshape(images.shape[0] * images.shape[1], images.shape[2])


def project(images, matrix):
    product = jnp.dot(flatten_rows(images), matrix, preferred_element_type=jnp.float32)
    return product.reshape(images.shape[0], images.shape[1], matrix.shape[1])


def project_back(grads, matrix):
    product = lax.dot_general(
        flatten_rows(grads), matrix, (((1,), (1,)), ((), ())), preferred_element_type=jnp.float32
    )
    return product.reshape(grads.shape[0], grads.shape[1], matrix.shape[0])


def outer_rows(left, right):
    return lax.dot_general(
        flatten_rows(left),
        flatten_rows(right),
        (((0,), (0,)), ((), ())),
        preferred_element_type=jnp.float32,
    )


def padded_grid(images, side):
    grid = images.reshape(images.shape[0], side, side, images.shape[2])
    return jnp.pad(grid, ((0, 0), (1, 1), (1, 1), (0, 0)))


def conv_same(images, kernel, side):
    padded = padded_grid(images, side)
    total = jnp.zeros((images.shape[0] * side * side, kernel.shape[2]), jnp.float32)
    for row in range(3):
        for column in range(3):
            window = padded[:, row : row + side, column : column + side, :].reshape(
                -1, images.shape[2]
            )
            total = total + jnp.dot(
                window, kernel[3 * row + column], preferred_element_type=jnp.float32
            )
    return total.reshape(images.shape[0], side * side, kernel.shape[2])


def conv_same_back(grads, kernel, side):
    padded = padded_grid(grads, side)
    total = jnp.zeros((grads.shape[0] * side * side, kernel.shape[1]), jnp.float32)
    for row in range(3):
        for column in range(3):
            window = padded[:, 2 - row : 2 - row + side, 2 - column : 2 - column + side, :].reshape(
                -1, grads.shape[2]
            )
            total = total + lax.dot_general(
                window,
                kernel[3 * row + column],
                (((1,), (1,)), ((), ())),
                preferred_element_type=jnp.float32,
            )
    return total.reshape(grads.shape[0], side * side, kernel.shape[1])


def conv_same_weight(images, grads, side):
    padded = padded_grid(images, side)
    flat = flatten_rows(grads)
    terms = []
    for row in range(3):
        for column in range(3):
            window = padded[:, row : row + side, column : column + side, :].reshape(
                -1, images.shape[2]
            )
            terms.append(
                lax.dot_general(
                    window, flat, (((0,), (0,)), ((), ())), preferred_element_type=jnp.float32
                )
            )
    return jnp.stack(terms)


def conv_half_back(grads, kernel, side):
    half = side // 2
    count = grads.shape[0]
    flat = flatten_rows(grads)
    canvas = None
    for row in range(3):
        for column in range(3):
            term = lax.dot_general(
                flat,
                kernel[3 * row + column],
                (((1,), (1,)), ((), ())),
                preferred_element_type=jnp.float32,
            )
            term = term.reshape(count, half, half, kernel.shape[1])
            placed = lax.pad(
                term,
                jnp.zeros((), term.dtype),
                ((0, 0, 0), (row, 3 - row, 1), (column, 3 - column, 1), (0, 0, 0)),
            )
            canvas = placed if canvas is None else canvas + placed
    return canvas[:, 1 : side + 1, 1 : side + 1, :].reshape(count, side * side, kernel.shape[1])


def conv_half_weight(images, grads, side):
    padded = padded_grid(images, side)
    flat = flatten_rows(grads)
    terms = []
    for row in range(3):
        for column in range(3):
            window = padded[:, row : row + side : 2, column : column + side : 2, :].reshape(
                -1, images.shape[2]
            )
            terms.append(
                lax.dot_general(
                    window, flat, (((0,), (0,)), ((), ())), preferred_element_type=jnp.float32
                )
            )
    return jnp.stack(terms)


def gather_outer(shard):
    return lax.all_gather(shard, "cout", axis=2, tiled=True)


def gather_inner(shard):
    return lax.all_gather(shard, "cin", axis=2, tiled=True)


def sum_inner(partial_value):
    return lax.psum_scatter(partial_value, "cin", scatter_dimension=2, tiled=True)


def sum_outer(partial_value):
    return lax.psum_scatter(partial_value, "cout", scatter_dimension=2, tiled=True)


def shards(
    inner_features,
    block_input,
    first_kernel,
    expand_weight,
    reduce_weight,
    stride_kernel,
    output_grad,
):
    feature_block = gather_outer(inner_features)
    first_hidden = sum_inner(conv_same(feature_block, first_kernel, SIDE))
    first_act = smooth_gate(first_hidden).astype(jnp.bfloat16)
    first_block = gather_inner(first_act)
    expanded = sum_outer(project(first_block, expand_weight))
    joined_pre = block_input.astype(jnp.float32) + expanded
    joined = smooth_gate(joined_pre).astype(jnp.bfloat16)
    joined_wide = gather_outer(joined)
    joined_pair = lax.all_to_all(joined_wide, "section", split_axis=2, concat_axis=0, tiled=True)
    hidden_part = project(joined_pair, reduce_weight)
    cotangent_block = gather_outer(output_grad)
    back_part = conv_half_back(cotangent_block, stride_kernel, SIDE)
    hidden_whole = lax.psum(hidden_part, ("section", "cin"))
    second_act = smooth_gate(hidden_whole).astype(jnp.bfloat16)
    back_whole = lax.psum(back_part, ("section", "cin"))
    masked_second = (back_whole * gate_slope(hidden_whole)).astype(jnp.bfloat16)
    stride_gradient = conv_half_weight(second_act, cotangent_block, SIDE)
    reduce_gradient = outer_rows(joined_pair, masked_second)
    joined_back = project_back(masked_second, reduce_weight)
    joined_home = lax.all_to_all(joined_back, "section", split_axis=0, concat_axis=2, tiled=True)
    back_joined = sum_outer(joined_home)
    input_gradient = (back_joined * gate_slope(joined_pre)).astype(jnp.bfloat16)
    input_wide = gather_outer(input_gradient)
    expand_local = outer_rows(first_block, input_wide)
    back_first = sum_inner(project_back(input_wide, expand_weight))
    masked_first = (back_first * gate_slope(first_hidden)).astype(jnp.bfloat16)
    masked_block = gather_inner(masked_first)
    inner_gradient = sum_outer(conv_same_back(masked_block, first_kernel, SIDE))
    first_local = conv_same_weight(feature_block, masked_block, SIDE)
    first_gradient, expand_gradient = (
        lax.psum(first_local.astype(jnp.bfloat16), "section").astype(jnp.float32),
        lax.psum(expand_local.astype(jnp.bfloat16), "section").astype(jnp.float32),
    )
    return (
        inner_gradient,
        input_gradient,
        first_gradient,
        expand_gradient,
        reduce_gradient,
        stride_gradient,
    )


def solution(mesh):
    return jax.shard_map(
        shards,
        mesh=mesh,
        in_specs=(
            P("section", None, ("cin", "cout")),
            P("section", None, ("cin", "cout")),
            P(None, "cin", "cout"),
            P("cout", "cin"),
            P(("cin", "section"), "cout"),
            P(None, "cout", ("section", "cin")),
            P(None, None, ("section", "cin", "cout")),
        ),
        out_specs=(
            P("section", None, ("cin", "cout")),
            P("section", None, ("cin", "cout")),
            P(None, "cin", "cout"),
            P("cout", "cin"),
            P(("cin", "section"), "cout"),
            P(None, "cout", ("section", "cin")),
        ),
        check_vma=False,
    )
```

profile of v0, /device:TPU:0, one launch (start us, length us, event | category | flops | bytes accessed | tf_op | source)
XLA Modules:
  0.0 957.9 jit_solution(9622084547646178098)
XLA Ops:
  7.2 30.3 %all_gather.19 = bf16[1,784,320]{1,2,0:T(8,128)(2,1)S(1)} all-gather(bf16[1,784,40]{1,2,0:T(8,128)(2,1)} %param.7), channel_id=1, replica_groups=mesh['section'=2,'cin'=8,'cout'=8] {'cout'}, dimensions={2}, use_global_device_ids=true | all-gather | bytes 564480 | tf_op jit(solution)/shard_map/all_gather | solution.py:137
  68.5 28.8 %all_gather.18 = bf16[2,196,320]{1,2,0:T(8,128)(2,1)S(1)} all-gather(bf16[2,196,40]{1,2,0:T(8,128)(2,1)S(1)} %copy-done.55), channel_id=1, replica_groups=mesh['section'=2,'cin'=8,'cout'=8] {'cout'}, dimensions={2}, use_global_device_ids=true | all-gather | bytes 282240 | tf_op jit(solution)/shard_map/all_gather | solution.py:137
  102.0 16.4 %pad.56 = f32[2,28,28,640]{3,2,1,0:T(8,128)} pad(f32[2,14,14,640]{3,2,1,0:T(8,128)} %fusion.54, f32[]{:T(128)} %constant.3.clone.1), padding=0_0_0x1_0_1x1_0_1x0_0_0 | pad | bytes 5017604 | tf_op jit(solution)/shard_map/slice | solution.py:116
  118.4 11.1 %pad.55 = f32[2,28,28,640]{3,2,1,0:T(8,128)} pad(f32[2,14,14,640]{3,2,1,0:T(8,128)S(1)} %fusion.56, f32[]{:T(128)} %constant.3.clone.1), padding=0_0_0x1_0_1x0_1_1x0_0_0 | pad | bytes 5017604 | tf_op jit(solution)/shard_map/slice | solution.py:116
  131.0 11.1 %pad.53 = f32[2,28,28,640]{3,2,1,0:T(8,128)} pad(f32[2,14,14,640]{3,2,1,0:T(8,128)S(1)} %fusion.60, f32[]{:T(128)} %constant.3.clone.1), padding=0_0_0x0_1_1x1_0_1x0_0_0 | pad | bytes 5017604 | tf_op jit(solution)/shard_map/slice | solution.py:116
  143.6 11.1 %pad.52 = f32[2,28,28,640]{3,2,1,0:T(8,128)} pad(f32[2,14,14,640]{3,2,1,0:T(8,128)S(1)} %fusion.62, f32[]{:T(128)} %constant.3.clone.1), padding=0_0_0x0_1_1x0_1_1x0_0_0 | pad | bytes 5017604 | tf_op jit(solution)/shard_map/slice | solution.py:116
  156.2 11.3 %pad.41 = f32[2,30,30,640]{3,2,1,0:T(8,128)} pad(f32[2,14,14,640]{3,2,1,0:T(8,128)S(1)} %fusion.66, f32[]{:T(128)} %constant.3.clone.1), padding=0_0_0x0_3_1x2_1_1x0_0_0 | pad | bytes 5611524 | tf_op jit(solution)/shard_map/pad | solution.py:110
  168.9 11.2 %pad.39 = f32[2,30,30,640]{3,2,1,0:T(8,128)} pad(f32[2,14,14,640]{3,2,1,0:T(8,128)S(1)} %fusion.70, f32[]{:T(128)} %constant.3.clone.1), padding=0_0_0x0_3_1x0_3_1x0_0_0 | pad | bytes 5611524 | tf_op jit(solution)/shard_map/pad | solution.py:110
  181.6 11.3 %pad.40 = f32[2,30,30,640]{3,2,1,0:T(8,128)} pad(f32[2,14,14,640]{3,2,1,0:T(8,128)S(1)} %fusion.68, f32[]{:T(128)} %constant.3.clone.1), padding=0_0_0x0_3_1x1_2_1x0_0_0 | pad | bytes 5611524 | tf_op jit(solution)/shard_map/pad | solution.py:110
  194.4 11.1 %pad.74 = f32[2,28,29,640]{3,2,1,0:T(8,128)} pad(f32[2,14,14,640]{3,2,1,0:T(8,128)S(1)} %fusion.64, f32[]{:T(128)} %constant.3.clone.1), padding=0_0_0x0_1_1x0_2_1x0_0_0 | pad | bytes 5160964
  207.0 11.2 %pad.73 = f32[2,28,29,640]{3,2,1,0:T(8,128)} pad(f32[2,14,14,640]{3,2,1,0:T(8,128)S(1)} %fusion.58, f32[]{:T(128)} %constant.3.clone.1), padding=0_0_0x1_0_1x0_2_1x0_0_0 | pad | bytes 5160964
  219.1 36.6 %all_gather.20 = bf16[1,784,320]{1,2,0:T(8,128)(2,1)S(1)} all-gather(bf16[1,784,40]{1,2,0:T(8,128)(2,1)S(1)} %multiply_convert_fusion.4), channel_id=1, replica_groups=mesh['section'=2,'cin'=8,'cout'=8] {'cin'}, dimensions={2}, use_global_device_ids=true | all-gather | bytes 564480 | tf_op jit(solution)/shard_map/all_gather | solution.py:141
  257.3 4.1 copy.97
  261.8 6.8 add_add_fusion
  268.6 11.1 %fusion.4 = f32[2,28,28,640]{3,2,1,0:T(8,128)S(1)} fusion(f32[2,28,28,640]{3,2,1,0:T(8,128)} %pad.56, f32[2,28,28,640]{3,2,1,0:T(8,128)} %pad.55, f32[2,28,28,640]{3,2,1,0:T(8,128)} %pad.53, f32[2,28,28,640]{3,2,1,0:T(8,128)} %pad.52, f32[2,30,30,640]{3,2,1,0:T(8,128)S(1)} %add_add_fusion, f32[2,28,29,640]{3,2,1,0:T(8,128)} %pad.74, f32[2,28,29,640]{3,2,1,0:T(8,128)} %pad.73), kind=kLoop, calls=%fused_computation.6 | loop fusion | flops 6021120 | bytes 32112640 | tf_op jit(solution)/shard_map/add | solution.py:115
  286.3 58.8 %all-reduce.24.cloned.1.call-done = f32[1,784,640]{1,0,2:T(1,128)} async-done(((f32[1,784,640]{1,0,2:T(1,128)}), f32[1,784,640]{1,0,2:T(1,128)}) %all-reduce.24.cloned.1.call-update) | async-done | bytes 2007056
  346.9 31.0 %all_gather.21 = bf16[1,784,640]{1,2,0:T(8,128)(2,1)S(1)} all-gather(bf16[1,784,80]{1,2,0:T(8,128)(2,1)S(1)} %multiply_convert_fusion.2), channel_id=1, replica_groups=mesh['section'=2,'cin'=8,'cout'=8] {'cout'}, dimensions={2}, use_global_device_ids=true | all-gather | bytes 1128960 | tf_op jit(solution)/shard_map/all_gather | solution.py:137
  380.2 9.0 reduce
  392.2 4.7 all_to_all.33
  404.7 195.4 %all-reduce.28.cloned.1.call-done = (f32[2,784,640]{2,1,0:T(8,128)}, f32[2,784,640]{2,1,0:T(8,128)}) async-done(((f32[2,784,640]{2,1,0:T(8,128)}, f32[2,784,640]{2,1,0:T(8,128)}), (f32[2,784,640]{2,1,0:T(8,128)}, f32[2,784,640]{2,1,0:T(8,128)})) %all-reduce.28.cloned.1.call-update) | async-done | bytes 8028176 | tf_op jit(solution)/shard_map/psum | solution.py:175
  600.2 5.1 multiply_convert_fusion
  606.6 5.6 all_to_all.34
  612.2 3.7 copy.100
  616.0 83.4 %all-reduce.26.cloned.1.call-done = f32[1,784,640]{1,0,2:T(1,128)} async-done(((f32[1,784,640]{1,0,2:T(1,128)}), f32[1,784,640]{1,0,2:T(1,128)}) %all-reduce.26.cloned.1.call-update) | async-done | bytes 2007056
  700.6 30.6 %all_gather.22 = bf16[1,784,640]{1,2,0:T(8,128)(2,1)S(1)} all-gather(bf16[1,784,80]{1,2,0:T(8,128)(2,1)S(1)} %fusion.85), channel_id=1, replica_groups=mesh['section'=2,'cin'=8,'cout'=8] {'cout'}, dimensions={2}, use_global_device_ids=true | all-gather | bytes 1128960 | tf_op jit(solution)/shard_map/all_gather | solution.py:137
  736.7 3.6 reshape.211
  741.9 5.0 fusion.137
  756.3 45.9 %reduce-scatter.16.cloned.1.call-done = f32[1,784,40]{1,2,0:T(8,128)} async-done(((f32[1,784,320]{1,2,0:T(8,128)}), f32[1,784,40]{1,2,0:T(8,128)}) %reduce-scatter.16.cloned.1.call-update) | async-done | bytes 125456
  803.2 35.5 %all_gather.23 = bf16[1,784,320]{1,2,0:T(8,128)(2,1)S(1)} all-gather(bf16[1,784,40]{1,2,0:T(8,128)(2,1)S(1)} %multiply_convert_fusion.3), channel_id=1, replica_groups=mesh['section'=2,'cin'=8,'cout'=8] {'cin'}, dimensions={2}, use_global_device_ids=true | all-gather | bytes 564480 | tf_op jit(solution)/shard_map/all_gather | solution.py:141
  841.3 6.5 pad_slice_fusion.4
  906.7 4.1 convert_element_type.43
  911.7 38.9 %reduce-scatter.18.cloned.1.call-done = f32[1,784,40]{1,2,0:T(8,128)} async-done(((f32[1,784,320]{1,2,0:T(8,128)}), f32[1,784,40]{1,2,0:T(8,128)}) %reduce-scatter.18.cloned.1.call-update) | async-done | bytes 125456
  (240 shorter events, 151.7 us)
Async XLA Ops:
  7.2 394.1 %copy-start = (bf16[320,640]{1,0:T(8,128)(2,1)S(1)}, bf16[320,640]{1,0:T(8,128)(2,1)}, u32[]{:S(2)}) copy-start(bf16[320,640]{1,0:T(8,128)(2,1)} %param.11) | copy-start | bytes 1228804
  7.2 211.0 %reduce-scatter.14.cloned.1.call-start = ((), (), s32[]{:S(2)}) async-start(), calls=%async_computation.7 | async-start | bytes 1290240
  42.1 6.6 copy-start.1
  68.4 276.6 %all-reduce.24.cloned.1.call-start = ((), (), s32[]{:S(2)}) async-start(), calls=%async_computation.5 | async-start | bytes 4587520
  206.9 49.6 %copy-start.48 = (bf16[320,640]{1,0:T(8,128)(2,1)S(1)}, bf16[320,640]{1,0:T(8,128)(2,1)}, u32[]{:S(2)}) copy-start(bf16[320,640]{1,0:T(8,128)(2,1)} %param.10) | copy-start | bytes 1228804
  261.5 338.7 %all-reduce.28.cloned.1.call-start = ((), (), s32[]{:S(2)}) async-start(), calls=%async_computation.10 | async-start | bytes 16056320 | tf_op jit(solution)/shard_map/psum | solution.py:175
  282.8 63.3 %copy-start.52 = (bf16[1,784,80]{1,2,0:T(8,128)(2,1)S(1)}, bf16[1,784,80]{1,2,0:T(8,128)(2,1)}, u32[]{:S(2)}) copy-start(bf16[1,784,80]{1,2,0:T(8,128)(2,1)} %param.8) | copy-start | bytes 376324
  404.7 294.7 %all-reduce.26.cloned.1.call-start = ((), (), s32[]{:S(2)}) async-start(), calls=%async_computation.6 | async-start | bytes 4587520
  615.9 84.6 %copy-start.15 = (f32[1,784,80]{1,0,2:T(1,128)S(1)}, f32[1,784,80]{1,0,2:T(1,128)}, u32[]{:S(2)}) copy-start(f32[1,784,80]{1,0,2:T(1,128)} %copy-done.14) | copy-start | bytes 752644
  615.9 116.3 %copy-start.49 = (bf16[320,640]{1,0:T(8,128)(2,1)S(1)}, bf16[320,640]{1,0:T(8,128)(2,1)}, u32[]{:S(2)}) copy-start(bf16[320,640]{1,0:T(8,128)(2,1)} %param.10) | copy-start | bytes 1228804
  615.9 186.3 %reduce-scatter.16.cloned.1.call-start = ((), (), s32[]{:S(2)}) async-start(), calls=%async_computation.8 | async-start | bytes 1290240
  700.6 33.3 %copy-start.51 = (bf16[1,784,80]{1,2,0:T(8,128)(2,1)}, bf16[1,784,80]{1,2,0:T(8,128)(2,1)S(1)}, u32[]{:S(2)}) copy-start(bf16[1,784,80]{1,2,0:T(8,128)(2,1)S(1)} %fusion.85) | copy-start | bytes 376324
  733.9 172.8 %all-reduce.30.cloned.1.call-start = ((), (), s32[]{:S(2)}) async-start(), calls=%async_computation.11 | async-start | bytes 5242880 | tf_op jit(solution)/shard_map/psum | solution.py:191
  736.7 3.6 copy-start.5
  748.9 5.8 copy-start.10
  749.9 4.9 copy-start.36
  752.3 49.9 %copy-start.53 = (f32[1,784,40]{1,2,0:T(8,128)S(1)}, f32[1,784,40]{1,2,0:T(8,128)}, u32[]{:S(2)}) copy-start(f32[1,784,40]{1,2,0:T(8,128)} %reduce-scatter.14.cloned.1.call-done) | copy-start | bytes 376324
  754.8 84.3 %copy-start.27 = (bf16[784,320]{1,0:T(8,128)(2,1)S(1)}, bf16[784,320]{1,0:T(8,128)(2,1)}, u32[]{:S(2)}) copy-start(bf16[784,320]{1,0:T(8,128)(2,1)} %reshape.186) | copy-start | bytes 1505284
  841.3 8.6 copy-start.2
  867.7 5.2 copy-start.7
  867.7 5.2 copy-start.17
  870.3 5.0 copy-start.26
  872.9 3.7 copy-start.25
  874.1 3.7 copy-start.21
  875.3 3.8 copy-start.23
  880.4 70.2 %reduce-scatter.18.cloned.1.call-start = ((), (), s32[]{:S(2)}) async-start(), calls=%async_computation.9 | async-start | bytes 1290240
  893.2 3.7 copy-start.45
  895.6 4.1 copy-start.46
  896.9 4.1 copy-start.47
  898.3 4.1 copy-start.4
  898.3 4.1 copy-start.50
  906.7 4.1 copy-start.54
  (32 other events, 46.4 us)
Sparse Core Ops, SparseCore 0:
  68.6 69.3 reduce-scatter.13
  261.6 83.4 all-reduce.23
  404.8 195.3 all-reduce.27
  616.1 83.3 all-reduce.25
  734.0 68.1 reduce-scatter.15
  880.6 26.0 all-reduce.29
  909.6 40.9 reduce-scatter.17
where the time goes:
time: 967 us; the launch traced here: 958 us
  waiting for transfers between devices  425 us (44%)
  local copies, waits for them, and re-layouts  203 us (21%)
  blocking collectives  203 us (21%)
  matrix products  70.4 us (7%)
  other arithmetic  39.2 us (4%)
  between operations  15.9 us (2%)
    unnamed x12, waiting for transfers between devices  227 us
    psum x1, waiting for transfers between devices, shards(): back_whole = lax.psum(back_part, ('section', 'cin'))  195 us
    all_gather x4, blocking collectives, gather_outer(): return lax.all_gather(shard, 'cout', axis=2, tiled=True)  121 us
    all_gather x2, blocking collectives, gather_inner(): return lax.all_gather(shard, 'cin', axis=2, tiled=True)  72.1 us
    slice x5, local copies, waits for them, and re-layouts, conv_half_back(): canvas[:, 1:side + 1, 1:side + 1, :]  52.9 us
    unnamed x123, local copies, waits for them, and re-layouts  39.9 us
    pad x3, local copies, waits for them, and re-layouts, conv_half_back(): lax.pad(term, jnp.zeros((), term.dtype), ((0, 0, 0), (row, 3 - row, 1), (...  33.8 us
  transfers between devices with their start and end apart: 7, of which 6 were waited for; matrix products, arithmetic and copies ran while one was open for 20% of the time, Pallas kernels for 0%

commit v1 on v0

--- a/solution.py
+++ b/solution.py
@@ -172,7 +172,7 @@
     back_part = conv_half_back(cotangent_block, stride_kernel, SIDE)
     hidden_whole = lax.psum(hidden_part, ("section", "cin"))
     second_act = smooth_gate(hidden_whole).astype(jnp.bfloat16)
-    back_whole = lax.psum(back_part, ("section", "cin"))
+    back_whole = jnp.sum(lax.all_gather(back_part, ("section", "cin")), axis=0)
     masked_second = (back_whole * gate_slope(hidden_whole)).astype(jnp.bfloat16)
     stride_gradient = conv_half_weight(second_act, cotangent_block, SIDE)
     reduce_gradient = outer_rows(joined_pair, masked_second)

time: 967 us -> 1180 us (1.22)
  waiting for transfers between devices: 425 us -> 614 us
  other arithmetic: 39.2 us -> 62.6 us
    all_gather x0 -> x1, waiting for transfers between devices: none -> 240 us  [shards(): back_whole = jnp.sum(lax.all_gather(back_part, ('section', 'cin')), axis=0)]
    psum x1, waiting for transfers between devices: 195 us -> 144 us  [shards(): hidden_whole = lax.psum(hidden_part, ('section', 'cin'))]
    reduce_sum x0 -> x1, other arithmetic: none -> 22.4 us  [shards(): back_whole = jnp.sum(lax.all_gather(back_part, ('section', 'cin')), axis=0)]
    unnamed x123 -> x109, local copies, waits for them, and re-layouts: 39.9 us -> 41.7 us
    unnamed x12 -> x13, waiting for transfers between devices: 227 us -> 227 us
  transfers between devices with their start and end apart: 7 -> 8, of which waited for: 6 -> 7; matrix products, arithmetic and copies ran while one was open for 20% -> 20% of each run, Pallas kernels for 0% -> 0%
where the time goes in v1:
time: 1180 us; the launch traced here: 1170 us
  waiting for transfers between devices  614 us (52%)
  blocking collectives  203 us (17%)
  local copies, waits for them, and re-layouts  199 us (17%)
  matrix products  70.7 us (6%)
  other arithmetic  62.6 us (5%)
  between operations  17.4 us (1%)
    all_gather x1, waiting for transfers between devices, shards(): back_whole = jnp.sum(lax.all_gather(back_part, ('section', 'cin')), axis=0)  240 us
    unnamed x13, waiting for transfers between devices  227 us
    psum x1, waiting for transfers between devices, shards(): hidden_whole = lax.psum(hidden_part, ('section', 'cin'))  144 us
    all_gather x4, blocking collectives, gather_outer(): return lax.all_gather(shard, 'cout', axis=2, tiled=True)  121 us
    all_gather x2, blocking collectives, gather_inner(): return lax.all_gather(shard, 'cin', axis=2, tiled=True)  72.2 us
    slice x5, local copies, waits for them, and re-layouts, conv_half_back(): canvas[:, 1:side + 1, 1:side + 1, :]  52.9 us
    unnamed x109, local copies, waits for them, and re-layouts  41.7 us
    pad x3, local copies, waits for them, and re-layouts, conv_half_back(): lax.pad(term, jnp.zeros((), term.dtype), ((0, 0, 0), (row, 3 - row, 1), (...  33.8 us
  transfers between devices with their start and end apart: 8, of which 7 were waited for; matrix products, arithmetic and copies ran while one was open for 20% of the time, Pallas kernels for 0%

profile of v1, /device:TPU:0, one launch (start us, length us, event | category | flops | bytes accessed | tf_op | source)
XLA Modules:
  0.0 1168.2 jit_solution(13536623778748939400)
XLA Ops:
  8.1 30.3 %all_gather.23 = bf16[1,784,320]{1,2,0:T(8,128)(2,1)S(1)} all-gather(bf16[1,784,40]{1,2,0:T(8,128)(2,1)} %param.7), channel_id=1, replica_groups=mesh['section'=2,'cin'=8,'cout'=8] {'cout'}, dimensions={2}, use_global_device_ids=true | all-gather | bytes 564480 | tf_op jit(solution)/shard_map/all_gather | solution.py:137
  39.7 6.2 pad_slice_fusion.8
  69.8 28.8 %all_gather.21 = bf16[2,196,320]{1,2,0:T(8,128)(2,1)S(1)} all-gather(bf16[2,196,40]{1,2,0:T(8,128)(2,1)S(1)} %copy-done.48), channel_id=1, replica_groups=mesh['section'=2,'cin'=8,'cout'=8] {'cout'}, dimensions={2}, use_global_device_ids=true | all-gather | bytes 282240 | tf_op jit(solution)/shard_map/all_gather | solution.py:137
  103.3 16.4 %pad.56 = f32[2,28,28,640]{3,2,1,0:T(8,128)} pad(f32[2,14,14,640]{3,2,1,0:T(8,128)} %fusion.54, f32[]{:T(128)} %constant.3.clone.1), padding=0_0_0x1_0_1x1_0_1x0_0_0 | pad | bytes 5017604 | tf_op jit(solution)/shard_map/slice | solution.py:116
  119.7 11.1 pad.55
  132.2 11.2 pad.73
  144.9 11.2 pad.53
  157.6 11.1 pad.52
  170.2 11.1 pad.74
  182.7 11.3 pad.39
  195.5 11.3 pad.41
  208.2 11.3 pad.40
  220.5 36.6 %all_gather.24 = bf16[1,784,320]{1,2,0:T(8,128)(2,1)S(1)} all-gather(bf16[1,784,40]{1,2,0:T(8,128)(2,1)S(1)} %multiply_convert_fusion.4), channel_id=1, replica_groups=mesh['section'=2,'cin'=8,'cout'=8] {'cin'}, dimensions={2}, use_global_device_ids=true | all-gather | bytes 564480 | tf_op jit(solution)/shard_map/all_gather | solution.py:141
  259.7 3.8 copy.99
  263.8 6.8 add_add_fusion
  270.6 11.1 fusion.4
  288.9 58.2 %all-reduce.25.cloned.1.call-done = f32[1,784,640]{1,0,2:T(1,128)} async-done(((f32[1,784,640]{1,0,2:T(1,128)}), f32[1,784,640]{1,0,2:T(1,128)}) %all-reduce.25.cloned.1.call-update) | async-done | bytes 2007056
  348.9 31.3 %all_gather.25 = bf16[1,784,640]{1,2,0:T(8,128)(2,1)S(1)} all-gather(bf16[1,784,80]{1,2,0:T(8,128)(2,1)S(1)} %multiply_convert_fusion.2), channel_id=1, replica_groups=mesh['section'=2,'cin'=8,'cout'=8] {'cout'}, dimensions={2}, use_global_device_ids=true | all-gather | bytes 1128960 | tf_op jit(solution)/shard_map/all_gather | solution.py:137
  382.4 9.0 reduce
  394.4 4.7 all_to_all.33
  407.0 239.9 %all-gather.2.cloned.1.call-done = f32[16,2,784,640]{3,2,1,0:T(8,128)} async-done(((f32[1,2,784,640]{3,2,1,0:T(8,128)}), f32[16,2,784,640]{3,2,1,0:T(8,128)}) %all-gather.2.cloned.1.call-update) | async-done | bytes 64225296 | tf_op jit(solution)/shard_map/all_gather | solution.py:175
  646.9 22.4 %reduce_sum.9 = f32[2,784,640]{2,1,0:T(8,128)} reduce(f32[16,2,784,640]{3,2,1,0:T(8,128)} %all-gather.2.cloned.1.call-done, f32[]{:T(128)} %constant.3.clone.1), dimensions={0}, to_apply=%region_0.1 | reduce | flops 15052800 | bytes 68239360 | tf_op jit(solution)/shard_map/reduce_sum | solution.py:175
  669.3 143.7 %all-reduce.23.cloned.1.call-done = f32[2,784,640]{2,1,0:T(8,128)} async-done(((f32[2,784,640]{2,1,0:T(8,128)}), f32[2,784,640]{2,1,0:T(8,128)}) %all-reduce.23.cloned.1.call-update) | async-done | bytes 4014096 | tf_op jit(solution)/shard_map/psum | solution.py:173
  813.0 5.1 multiply_convert_fusion
  819.4 5.6 all_to_all.34
  828.8 85.5 %all-reduce.27.cloned.1.call-done = f32[1,784,640]{1,0,2:T(1,128)} async-done(((f32[1,784,640]{1,0,2:T(1,128)}), f32[1,784,640]{1,0,2:T(1,128)}) %all-reduce.27.cloned.1.call-update) | async-done | bytes 2007056
  916.2 30.5 %all_gather.26 = bf16[1,784,640]{1,2,0:T(8,128)(2,1)S(1)} all-gather(bf16[1,784,80]{1,2,0:T(8,128)(2,1)S(1)} %fusion.85), channel_id=1, replica_groups=mesh['section'=2,'cin'=8,'cout'=8] {'cout'}, dimensions={2}, use_global_device_ids=true | all-gather | bytes 1128960 | tf_op jit(solution)/shard_map/all_gather | solution.py:137
  957.4 5.0 fusion.137
  971.8 45.9 %reduce-scatter.16.cloned.1.call-done = f32[1,784,40]{1,2,0:T(8,128)} async-done(((f32[1,784,320]{1,2,0:T(8,128)}), f32[1,784,40]{1,2,0:T(8,128)}) %reduce-scatter.16.cloned.1.call-update) | async-done | bytes 125456
  1018.7 35.6 %all_gather.27 = bf16[1,784,320]{1,2,0:T(8,128)(2,1)S(1)} all-gather(bf16[1,784,40]{1,2,0:T(8,128)(2,1)S(1)} %multiply_convert_fusion.3), channel_id=1, replica_groups=mesh['section'=2,'cin'=8,'cout'=8] {'cin'}, dimensions={2}, use_global_device_ids=true | all-gather | bytes 564480 | tf_op jit(solution)/shard_map/all_gather | solution.py:141
  1118.4 4.1 convert_element_type.43
  1122.5 37.8 %reduce-scatter.18.cloned.1.call-done = f32[1,784,40]{1,2,0:T(8,128)} async-done(((f32[1,784,320]{1,2,0:T(8,128)}), f32[1,784,40]{1,2,0:T(8,128)}) %reduce-scatter.18.cloned.1.call-update) | async-done | bytes 125456
  (230 shorter events, 157.3 us)
Async XLA Ops:
  8.0 395.6 %copy-start = (bf16[320,640]{1,0:T(8,128)(2,1)S(1)}, bf16[320,640]{1,0:T(8,128)(2,1)}, u32[]{:S(2)}) copy-start(bf16[320,640]{1,0:T(8,128)(2,1)} %param.11) | copy-start | bytes 1228804
  8.0 211.5 %reduce-scatter.14.cloned.1.call-start = ((), (), s32[]{:S(2)}) async-start(), calls=%async_computation.9 | async-start | bytes 1290240
  53.4 6.6 copy-start.1
  60.0 2.3 copy-start.25
  69.7 277.4 %all-reduce.25.cloned.1.call-start = ((), (), s32[]{:S(2)}) async-start(), calls=%async_computation.7 | async-start | bytes 4587520
  263.5 383.3 %all-gather.2.cloned.1.call-start = ((), (), s32[]{:S(2)}) async-start(), calls=%async_computation.5 | async-start | bytes 68239360 | tf_op jit(solution)/shard_map/all_gather | solution.py:175
  287.0 61.1 %copy-start.46 = (bf16[1,784,80]{1,2,0:T(8,128)(2,1)S(1)}, bf16[1,784,80]{1,2,0:T(8,128)(2,1)}, u32[]{:S(2)}) copy-start(bf16[1,784,80]{1,2,0:T(8,128)(2,1)} %param.8) | copy-start | bytes 376324
  287.1 525.9 %all-reduce.23.cloned.1.call-start = ((), (), s32[]{:S(2)}) async-start(), calls=%async_computation.6 | async-start | bytes 8028160 | tf_op jit(solution)/shard_map/psum | solution.py:173
  406.9 507.4 %all-reduce.27.cloned.1.call-start = ((), (), s32[]{:S(2)}) async-start(), calls=%async_computation.8 | async-start | bytes 4587520
  828.8 86.6 %copy-start.14 = (f32[1,784,80]{1,0,2:T(1,128)S(1)}, f32[1,784,80]{1,0,2:T(1,128)}, u32[]{:S(2)}) copy-start(f32[1,784,80]{1,0,2:T(1,128)} %copy-done.13) | copy-start | bytes 752644
  828.8 119.0 %copy-start.43 = (bf16[320,640]{1,0:T(8,128)(2,1)S(1)}, bf16[320,640]{1,0:T(8,128)(2,1)}, u32[]{:S(2)}) copy-start(bf16[320,640]{1,0:T(8,128)(2,1)} %param.10) | copy-start | bytes 1228804
  828.8 189.0 %reduce-scatter.16.cloned.1.call-start = ((), (), s32[]{:S(2)}) async-start(), calls=%async_computation.10 | async-start | bytes 1290240
  947.8 1.9 copy-start.12
  949.5 167.0 %all-reduce.29.cloned.1.call-start = ((), (), s32[]{:S(2)}) async-start(), calls=%async_computation.12 | async-start | bytes 5242880 | tf_op jit(solution)/shard_map/psum | solution.py:191
  952.2 3.6 copy-start.5
  964.5 5.8 copy-start.9
  965.4 4.9 copy-start.33
  967.9 49.9 %copy-start.47 = (f32[1,784,40]{1,2,0:T(8,128)S(1)}, f32[1,784,40]{1,2,0:T(8,128)}, u32[]{:S(2)}) copy-start(f32[1,784,40]{1,2,0:T(8,128)} %reduce-scatter.14.cloned.1.call-done) | copy-start | bytes 376324
  1054.3 13.9 %copy-start.6 = (bf16[1,784,320]{1,2,0:T(8,128)(2,1)}, bf16[1,784,320]{1,2,0:T(8,128)(2,1)S(1)}, u32[]{:S(2)}) copy-start(bf16[1,784,320]{1,2,0:T(8,128)(2,1)S(1)} %all_gather.27) | copy-start | bytes 1505284
  1057.1 4.8 copy-start.24
  1059.5 4.9 copy-start.22
  1061.9 3.7 copy-start.20
  1063.2 3.7 copy-start.18
  1064.4 3.8 copy-start.16
  1072.4 6.7 copy-start.2
  1090.2 70.0 %reduce-scatter.18.cloned.1.call-start = ((), (), s32[]{:S(2)}) async-start(), calls=%async_computation.11 | async-start | bytes 1290240
  1090.6 2.2 copy-start.30
  1099.7 2.0 copy-start.36
  1103.0 4.1 copy-start.42
  1104.4 4.1 copy-start.41
  1107.1 4.1 copy-start.4
  1107.1 4.1 copy-start.44
  (26 other events, 30.4 us)
Sparse Core Ops, SparseCore 0:
  69.8 69.3 reduce-scatter.13
  263.6 83.4 all-reduce.24
  828.9 85.3 all-reduce.26
  949.6 68.1 reduce-scatter.15
  1090.3 26.0 all-reduce.28
  1119.3 40.9 reduce-scatter.17
Sparse Core Ops, SparseCore 1:
  287.2 359.6 all-gather.1
  649.9 163.1 all-reduce.22
